TPU v7x, 32 devices: a whole 2x2x4 slice. The times are simulated.
32 devices in a mesh: rows: 16 (over z, x, core), cols: 2 (over y).
Axes of the slice: x: 2, y: 2, z: 4, core: 2. Of those that a mesh axis runs over, the one named last changes fastest.
Arguments:
- states: float32 [32, 16384], P('cols', 'rows'), may hold values from -120 to 120, as said below
- adj_weight: bfloat16 [128, 3, 128, 128], P('rows'), may hold values from 0.099609375 to 2
- adj_index: int32 [128, 3], P('rows'), may hold values from 0 to 127, as said below
- partner: int32 [128], P('rows'), may hold values from 0 to 127, as said below
Outputs:
- correction: float32 [32, 16384], P('cols', 'rows')
Inputs may be any that keep to these rules, and one draw needn't show every extreme that they name: adj_index[b, 0] = b; every other entry lies within 4 blocks of b. partner[partner[b]] = b and partner[b] != b; the 8 blocks of one index of rows have their partners on 8 different other indices of rows, at most one block on each. `states`: finite values.
All inputs are finite; a program needn't handle non-finite values.
Results may differ from a plain program's by a relative error of at most 0.0003.
Values sent between devices are 32-bit elements; how exact they have to be, the bound alone decides.
No kernel may reach another device: no remote copies, remote signals or barrier semaphores. Data moves between devices by JAX's collectives and lax.ppermute only.
A program may use at most 64 MiB of HBM per device.

v0:
```python
import jax
import jax.numpy as jnp
from jax import lax
from jax.sharding import PartitionSpec as P

DAMPING = 2.0 / 3.0
EPSILON = 1e-06
EXACT = lax.Precision.HIGHEST


def extended(shard, sides, width):
    for axis, dim in sides:
        peers, length = (lax.axis_size(axis), shard.shape[dim])
        up = [(i, (i + 1) % peers) for i in range(peers - 1)]
        down = [(j, i) for i, j in up]
        last = lax.slice_in_dim(shard, length - width, length, axis=dim)
        initial = lax.slice_in_dim(shard, 0, width, axis=dim)
        before = lax.ppermute(last, axis, up)
        after = lax.ppermute(initial, axis, down)
        shard = jnp.concatenate([before, shard, after], axis=dim)
    return shard


def to_slots(values, owner_dev, row_devices):
    empty = jnp.zeros((values.shape[0], row_devices, values.shape[2]), values.dtype)
    return empty.at[:, owner_dev].set(values)


def from_slots(arrived, owner_dev):
    return arrived[:, owner_dev]


def solve_ritz(gram_matrix, rayleigh):
    factor = jnp.linalg.cholesky(gram_matrix)
    return jax.scipy.linalg.cho_solve((factor, True), rayleigh)


def local(states, adj_weight, adj_index, partner):
    local_cols, vertices = states.shape
    blocks_here = adj_weight.shape[0]
    block_len = adj_weight.shape[2]
    row_devices = lax.axis_size("rows")
    margin_blocks = blocks_here // 2
    local_ids = adj_index - (lax.axis_index("rows") * blocks_here - margin_blocks)
    owner_dev = partner // blocks_here
    degree = jnp.sum(adj_weight, axis=(1, 3), dtype=jnp.float32).reshape(vertices)
    degree_blocks = degree.reshape(1, blocks_here, block_len)

    def operate(vector_in):
        widened = extended(vector_in, (("rows", 1),), margin_blocks * block_len)
        grid_blocks = widened.reshape(local_cols, -1, block_len)
        picked = grid_blocks[:, local_ids]
        neighbour = jnp.einsum(
            "bkij,cbkj->cbi",
            adj_weight,
            picked,
            precision=EXACT,
            preferred_element_type=jnp.float32,
        )
        return degree * vector_in - neighbour.reshape(local_cols, vertices)

    applied = operate(states)
    all_states = lax.all_gather(states, "cols", axis=0, tiled=True)
    gram_part = jnp.einsum("cv,dv->cd", all_states * degree, all_states, precision=EXACT)
    rayleigh_part = jnp.einsum("cv,dv->cd", all_states, applied, precision=EXACT)
    gram_matrix, rayleigh = lax.psum((gram_part, rayleigh_part), "rows")
    ritz_matrix = solve_ritz(gram_matrix, rayleigh)
    residual = applied - degree * jnp.einsum("cd,cv->dv", ritz_matrix, all_states, precision=EXACT)
    presmooth = DAMPING * residual / degree
    remain = (residual - operate(presmooth)).reshape(local_cols, blocks_here, block_len)
    arrived, arrived_degree = (
        lax.all_to_all(
            to_slots(remain, owner_dev, row_devices),
            "rows",
            split_axis=1,
            concat_axis=1,
            tiled=True,
        ),
        lax.all_to_all(
            to_slots(degree_blocks, owner_dev, row_devices),
            "rows",
            split_axis=1,
            concat_axis=1,
            tiled=True,
        ),
    )
    coarse_degree = (degree_blocks + from_slots(arrived_degree, owner_dev)).reshape(vertices)
    coarse = (remain + from_slots(arrived, owner_dev)).reshape(local_cols, vertices)
    coarse_fix = DAMPING * coarse / coarse_degree
    product = operate(coarse_fix).reshape(local_cols, blocks_here, block_len)
    arrived_product = lax.all_to_all(
        to_slots(product, owner_dev, row_devices), "rows", split_axis=1, concat_axis=1, tiled=True
    )
    coarse_image = (product + from_slots(arrived_product, owner_dev)).reshape(local_cols, vertices)
    coarse_fix = coarse_fix + DAMPING * (coarse - coarse_image) / coarse_degree
    second = presmooth + coarse_fix
    smooth = second + DAMPING * (residual - operate(second)) / degree
    squares = lax.psum(jnp.sum(smooth * smooth, axis=1), "rows")
    return smooth / jnp.sqrt(squares / (vertices * row_devices) + EPSILON)[:, None]


def solution(mesh):
    return jax.shard_map(
        local,
        mesh=mesh,
        in_specs=(P("cols", "rows"), P("rows", None, None, None), P("rows", None), P("rows")),
        out_specs=P("cols", "rows"),
        check_vma=False,
    )
```

profile of v0, /device:TPU:0, one launch (start us, length us, event | category | flops | bytes accessed | tf_op | source)
XLA Modules:
  0.0 170.4 jit_solution(17137495620325622604)
XLA Ops:
  0.0 0.8 fusion.28
  0.8 2.4 %collective-permute-start = (f32[16,512]{1,0:T(8,128)S(1)}, f32[16,512]{1,0:T(8,128)S(1)}, u32[]{:S(2)}, u32[]{:S(2)}) collective-permute-start(f32[16,512]{1,0:T(8,128)S(1)} %get-tuple-element.15), channel_id=1, source_target_pairs={{0,2},{2,4},{4,6},{6,8},{8,10},{10,12},{12,14},{14,16},{16,18},{18... | collective-permute-start | bytes 98312 | tf_op jit(solution)/shard_map/ppermute | solution.py:18
  3.2 1.3 collective-permute-start.1
  4.5 5.5 %all_gather.3 = f32[32,1024]{1,0:T(8,128)S(1)} all-gather(f32[16,1024]{1,0:T(8,128)} %param.4), channel_id=1, replica_groups=mesh['rows'=16,'cols'=2] {'cols'}, dimensions={0}, use_global_device_ids=true | all-gather | bytes 196608 | tf_op jit(solution)/shard_map/all_gather | solution.py:63
  10.1 0.7 compare_select_fusion
  10.9 1.4 convert_reduce_fusion
  13.3 0.9 convolution_bitcast_fusion.3
  14.4 62.2 %all-reduce = (f32[32,16]{0,1:T(8,128)S(1)}, f32[32,32]{0,1:T(8,128)S(1)}) all-reduce(f32[32,16]{0,1:T(8,128)S(1)} %convolution_bitcast_fusion.4, f32[32,32]{0,1:T(8,128)S(1)} %fusion.1), channel_id=1, replica_groups=mesh['rows'=16,'cols'=2] {'rows'}, use_global_device_ids=true, to_apply=%region_4.5 | all-reduce | flops 1536 | bytes 12288 | tf_op jit(solution)/shard_map/psum | solution.py:66
  76.7 2.9 %cholesky.16 = f32[32,32]{1,0:T(8,128)S(1)} custom-call(f32[32,32]{1,0:T(8,128)S(1)} %fusion.20), custom_call_target="Cholesky" | custom-call | tf_op jit(solution)/shard_map/jit(cholesky)/cholesky | solution.py:34
  80.3 0.7 fusion.15
  81.0 2.4 %custom-call.10 = f32[1,32,32]{1,2,0:T(8,128)S(1)} custom-call(f32[1,32,32]{2,1,0:T(8,128)S(1)} %fusion.15), custom_call_target="InvertDiagBlocksLowerTriangular" | custom-call | tf_op jit(solution)/shard_map/jit(_cho_solve)/triangular_solve | solution.py:35
  83.9 1.3 collective-permute-start.2
  85.2 1.3 collective-permute-start.3
  86.6 1.2 scatter_custom_fusion.1
  87.7 3.5 %all-to-all-start.1 = ((f32[1,16,128]{2,0,1:T(1,128)}), f32[1,16,128]{2,0,1:T(1,128)S(1)}, u32[]{:S(2)}, u32[]{:S(2)}) async-start(f32[1,16,128]{2,0,1:T(1,128)} %bitcast.17), calls=%async_computation.1 | async-start | bytes 16384 | tf_op jit(solution)/shard_map/all_to_all | solution.py:79
  91.8 0.9 convolution_bitcast_fusion.2
  93.4 2.0 %scatter_fusion = f32[16,16,128]{2,0,1:T(8,128)} fusion(f32[16,16,128]{2,0,1:T(8,128)} %broadcast.109.clone, s32[8]{0:T(128)S(1)} %compare_select_fusion.1, f32[8,16,128]{2,1,0:T(8,128)S(1)} %bitcast_bitcast_fusion.1), kind=kCustom, calls=%fused_computation.7 | custom fusion | bytes 196640 | tf_op jit(solution)/shard_map/scatter | solution.py:26
  95.4 2.1 %all-to-all-done.1 = f32[1,16,128]{2,0,1:T(1,128)S(1)} async-done(((f32[1,16,128]{2,0,1:T(1,128)}), f32[1,16,128]{2,0,1:T(1,128)S(1)}, u32[]{:S(2)}, u32[]{:S(2)}) %all-to-all-start.1) | async-done | bytes 8224 | tf_op jit(solution)/shard_map/all_to_all | solution.py:79
  97.5 3.9 %all-to-all-start = ((f32[16,16,128]{2,0,1:T(8,128)}), f32[16,16,128]{2,0,1:T(8,128)S(1)}, u32[]{:S(2)}, u32[]{:S(2)}) async-start(f32[16,16,128]{2,0,1:T(8,128)} %scatter_fusion), calls=%async_computation | async-start | bytes 262144 | tf_op jit(solution)/shard_map/all_to_all | solution.py:72
  102.0 7.3 %all-to-all-done = f32[16,16,128]{2,0,1:T(8,128)S(1)} async-done(((f32[16,16,128]{2,0,1:T(8,128)}), f32[16,16,128]{2,0,1:T(8,128)S(1)}, u32[]{:S(2)}, u32[]{:S(2)}) %all-to-all-start) | async-done | bytes 131104 | tf_op jit(solution)/shard_map/all_to_all | solution.py:72
  109.9 1.3 collective-permute-start.4
  111.2 1.3 collective-permute-start.5
  112.5 1.8 %collective-permute-done.5 = f32[16,512]{1,0:T(8,128)S(1)} collective-permute-done((f32[16,512]{1,0:T(8,128)S(1)}, f32[16,512]{1,0:T(8,128)S(1)}, u32[]{:S(2)}, u32[]{:S(2)}) %collective-permute-start.5) | collective-permute-done | bytes 32800 | tf_op jit(solution)/shard_map/ppermute | solution.py:19
  114.9 0.9 convolution_bitcast_fusion.1
  115.9 0.7 scatter_fusion.1
  116.6 14.6 %all_to_all.15 = f32[16,16,128]{2,0,1:T(8,128)S(1)} all-to-all(f32[16,16,128]{2,0,1:T(8,128)S(1)} %scatter_fusion.1), channel_id=1, replica_groups=mesh['rows'=16,'cols'=2] {'rows'}, dimensions={1} | all-to-all | bytes 262144 | tf_op jit(solution)/shard_map/all_to_all | solution.py:91
  131.9 1.3 collective-permute-start.6
  133.2 1.3 collective-permute-start.7
  134.5 1.8 %collective-permute-done.7 = f32[16,512]{1,0:T(8,128)S(1)} collective-permute-done((f32[16,512]{1,0:T(8,128)S(1)}, f32[16,512]{1,0:T(8,128)S(1)}, u32[]{:S(2)}, u32[]{:S(2)}) %collective-permute-start.7) | collective-permute-done | bytes 32800 | tf_op jit(solution)/shard_map/ppermute | solution.py:19
  136.9 0.9 convolution_bitcast_fusion
  137.9 31.7 %psum.23 = f32[16]{0:T(128)S(1)} all-reduce(f32[16]{0:T(128)S(1)} %get-tuple-element.7), channel_id=1, replica_groups=mesh['rows'=16,'cols'=2] {'rows'}, use_global_device_ids=true, to_apply=%region_9.10 | all-reduce | flops 16 | bytes 128 | tf_op jit(solution)/shard_map/psum | solution.py:98
  169.7 0.7 broadcast_divide_fusion
  (49 shorter events, 6.9 us)
Async XLA Ops:
  0.0 12.6 %copy-start.1 = (f32[16,1024]{1,0:T(8,128)S(1)}, f32[16,1024]{1,0:T(8,128)}, u32[]{:S(2)}) copy-start(f32[16,1024]{1,0:T(8,128)} %param.4) | copy-start | bytes 196612
  0.8 11.8 %collective-permute-start = (f32[16,512]{1,0:T(8,128)S(1)}, f32[16,512]{1,0:T(8,128)S(1)}, u32[]{:S(2)}, u32[]{:S(2)}) collective-permute-start(f32[16,512]{1,0:T(8,128)S(1)} %get-tuple-element.15), channel_id=1, source_target_pairs={{0,2},{2,4},{4,6},{6,8},{8,10},{10,12},{12,14},{14,16},{16,18},{18... | collective-permute-start | bytes 98312 | tf_op jit(solution)/shard_map/ppermute | solution.py:18
  3.2 9.4 %collective-permute-start.1 = (f32[16,512]{1,0:T(8,128)S(1)}, f32[16,512]{1,0:T(8,128)S(1)}, u32[]{:S(2)}, u32[]{:S(2)}) collective-permute-start(f32[16,512]{1,0:T(8,128)S(1)} %get-tuple-element.16), channel_id=1, source_target_pairs={{2,0},{4,2},{6,4},{8,6},{10,8},{12,10},{14,12},{16,14},{18,16},{20... | collective-permute-start | bytes 98312 | tf_op jit(solution)/shard_map/ppermute | solution.py:19
  10.9 2.3 %copy-start = (bf16[8,3,128,128]{3,2,1,0:T(8,128)(2,1)S(1)}, bf16[8,3,128,128]{3,2,1,0:T(8,128)(2,1)}, u32[]{:S(2)}) copy-start(bf16[8,3,128,128]{3,2,1,0:T(8,128)(2,1)} %param.5) | copy-start | bytes 2359300
  14.2 72.4 %copy-start.2 = (s32[8]{0:T(128)S(1)}, s32[8]{0:T(128)}, u32[]{:S(2)}) copy-start(s32[8]{0:T(128)} %param.7) | copy-start | bytes 100
  83.9 7.3 %collective-permute-start.2 = (f32[16,512]{1,0:T(8,128)S(1)}, f32[16,512]{1,0:T(8,128)S(1)}, u32[]{:S(2)}, u32[]{:S(2)}) collective-permute-start(f32[16,512]{1,0:T(8,128)S(1)} %get-tuple-element.13), channel_id=1, source_target_pairs={{0,2},{2,4},{4,6},{6,8},{8,10},{10,12},{12,14},{14,16},{16,18},{18... | collective-permute-start | bytes 98312 | tf_op jit(solution)/shard_map/ppermute | solution.py:18
  85.2 6.0 %collective-permute-start.3 = (f32[16,512]{1,0:T(8,128)S(1)}, f32[16,512]{1,0:T(8,128)S(1)}, u32[]{:S(2)}, u32[]{:S(2)}) collective-permute-start(f32[16,512]{1,0:T(8,128)S(1)} %get-tuple-element.14), channel_id=1, source_target_pairs={{2,0},{4,2},{6,4},{8,6},{10,8},{12,10},{14,12},{16,14},{18,16},{20... | collective-permute-start | bytes 98312 | tf_op jit(solution)/shard_map/ppermute | solution.py:19
  87.7 9.8 %all-to-all-start.1 = ((f32[1,16,128]{2,0,1:T(1,128)}), f32[1,16,128]{2,0,1:T(1,128)S(1)}, u32[]{:S(2)}, u32[]{:S(2)}) async-start(f32[1,16,128]{2,0,1:T(1,128)} %bitcast.17), calls=%async_computation.1 | async-start | bytes 16384 | tf_op jit(solution)/shard_map/all_to_all | solution.py:79
  97.5 11.8 %all-to-all-start = ((f32[16,16,128]{2,0,1:T(8,128)}), f32[16,16,128]{2,0,1:T(8,128)S(1)}, u32[]{:S(2)}, u32[]{:S(2)}) async-start(f32[16,16,128]{2,0,1:T(8,128)} %scatter_fusion), calls=%async_computation | async-start | bytes 262144 | tf_op jit(solution)/shard_map/all_to_all | solution.py:72
  109.9 2.6 %collective-permute-start.4 = (f32[16,512]{1,0:T(8,128)S(1)}, f32[16,512]{1,0:T(8,128)S(1)}, u32[]{:S(2)}, u32[]{:S(2)}) collective-permute-start(f32[16,512]{1,0:T(8,128)S(1)} %get-tuple-element.11), channel_id=1, source_target_pairs={{0,2},{2,4},{4,6},{6,8},{8,10},{10,12},{12,14},{14,16},{16,18},{18... | collective-permute-start | bytes 98312 | tf_op jit(solution)/shard_map/ppermute | solution.py:18
  111.2 3.1 %collective-permute-start.5 = (f32[16,512]{1,0:T(8,128)S(1)}, f32[16,512]{1,0:T(8,128)S(1)}, u32[]{:S(2)}, u32[]{:S(2)}) collective-permute-start(f32[16,512]{1,0:T(8,128)S(1)} %get-tuple-element.12), channel_id=1, source_target_pairs={{2,0},{4,2},{6,4},{8,6},{10,8},{12,10},{14,12},{16,14},{18,16},{20... | collective-permute-start | bytes 98312 | tf_op jit(solution)/shard_map/ppermute | solution.py:19
  131.9 2.6 %collective-permute-start.6 = (f32[16,512]{1,0:T(8,128)S(1)}, f32[16,512]{1,0:T(8,128)S(1)}, u32[]{:S(2)}, u32[]{:S(2)}) collective-permute-start(f32[16,512]{1,0:T(8,128)S(1)} %get-tuple-element.9), channel_id=1, source_target_pairs={{0,2},{2,4},{4,6},{6,8},{8,10},{10,12},{12,14},{14,16},{16,18},{18... | collective-permute-start | bytes 98312 | tf_op jit(solution)/shard_map/ppermute | solution.py:18
  133.2 3.1 %collective-permute-start.7 = (f32[16,512]{1,0:T(8,128)S(1)}, f32[16,512]{1,0:T(8,128)S(1)}, u32[]{:S(2)}, u32[]{:S(2)}) collective-permute-start(f32[16,512]{1,0:T(8,128)S(1)} %get-tuple-element.10), channel_id=1, source_target_pairs={{2,0},{4,2},{6,4},{8,6},{10,8},{12,10},{14,12},{16,14},{18,16},{20... | collective-permute-start | bytes 98312 | tf_op jit(solution)/shard_map/ppermute | solution.py:19
where the time goes:
time: 171 us; the launch traced here: 170 us
  blocking collectives  114 us (67%)
  starting transfers between devices  18.8 us (11%)
  waiting for transfers between devices  13 us (8%)
  other arithmetic  9.87 us (6%)
  local copies, waits for them, and re-layouts  9.62 us (6%)
  matrix products  4.63 us (3%)
    psum x1, blocking collectives, local(): gram_matrix, rayleigh = lax.psum((gram_part, rayleigh_part), 'rows')  62.2 us
    psum x1, blocking collectives, local(): squares = lax.psum(jnp.sum(smooth * smooth, axis=1), 'rows')  31.7 us
    all_to_all x1, blocking collectives, local(): lax.all_to_all(to_slots(product, owner_dev, row_devices), 'rows', split_a...  14.6 us
    all_to_all x1, waiting for transfers between devices, local(): lax.all_to_all(to_slots(remain, owner_dev, row_devices), 'rows', split_ax...  7.32 us
    ppermute x4, starting transfers between devices, extended(): before = lax.ppermute(last, axis, up)  6.26 us
    all_gather x1, blocking collectives, local(): all_states = lax.all_gather(states, 'cols', axis=0, tiled=True)  5.51 us
    ppermute x4, starting transfers between devices, extended(): after = lax.ppermute(initial, axis, down)  5.17 us
    scatter x3, local copies, waits for them, and re-layouts, to_slots(): return empty.at[:, owner_dev].set(values)  3.89 us
  transfers between devices with their start and end apart: 10, of which 4 were waited for; matrix products, arithmetic and copies ran while one was open for 5% of the time, Pallas kernels for 0%

commit v1 on v0

--- a/solution.py
+++ b/solution.py
@@ -6,6 +6,18 @@
 DAMPING = 2.0 / 3.0
 EPSILON = 1e-06
 EXACT = lax.Precision.HIGHEST
+
+
+def rotated_exchange(x, axis, split, join):
+    ways, here = (lax.axis_size(axis), lax.axis_index(axis))
+    width = x.shape[split] // ways
+    turned = jnp.roll(x, -here * width, axis=split)
+    got = [lax.slice_in_dim(turned, 0, width, axis=split)]
+    for far in range(1, ways):
+        sent = lax.slice_in_dim(turned, far * width, (far + 1) * width, axis=split)
+        got.append(lax.ppermute(sent, axis, [(d, (d + far) % ways) for d in range(ways)]))
+    line = jnp.concatenate(got[::-1], axis=join)
+    return jnp.roll(line, (here + 1) * got[0].shape[join], axis=join)
 
 
 def extended(shard, sides, width):
@@ -88,9 +100,7 @@
     coarse = (remain + from_slots(arrived, owner_dev)).reshape(local_cols, vertices)
     coarse_fix = DAMPING * coarse / coarse_degree
     product = operate(coarse_fix).reshape(local_cols, blocks_here, block_len)
-    arrived_product = lax.all_to_all(
-        to_slots(product, owner_dev, row_devices), "rows", split_axis=1, concat_axis=1, tiled=True
-    )
+    arrived_product = rotated_exchange(to_slots(product, owner_dev, row_devices), "rows", 1, 1)
     coarse_image = (product + from_slots(arrived_product, owner_dev)).reshape(local_cols, vertices)
     coarse_fix = coarse_fix + DAMPING * (coarse - coarse_image) / coarse_degree
     second = presmooth + coarse_fix

time: 171 us -> 218 us (1.27)
  starting transfers between devices: 18.8 us -> 59.6 us
  waiting for transfers between devices: 13 us -> 33.4 us
  blocking collectives: 114 us -> 99.9 us
    ppermute x0 -> x15, starting transfers between devices: none -> 40.8 us  [rotated_exchange(): lax.ppermute(sent, axis, [(d, (d + far) % ways) for d in range(ways)])]
    ppermute x0 -> x15, waiting for transfers between devices: none -> 17.3 us  [rotated_exchange(): lax.ppermute(sent, axis, [(d, (d + far) % ways) for d in range(ways)])]
    all_to_all x1 -> x0, blocking collectives: 14.6 us -> none  [local(): lax.all_to_all(to_slots(product, owner_dev, row_devices), 'rows', split_a...]
    ppermute x4, waiting for transfers between devices: 3.59 us -> 6.72 us  [extended(): after = lax.ppermute(initial, axis, down)]
  transfers between devices with their start and end apart: 10 -> 25, of which waited for: 4 -> 14; matrix products, arithmetic and copies ran while one was open for 5% -> 4% of each run, Pallas kernels for 0% -> 0%
where the time goes in v1:
time: 218 us
  blocking collectives  99.9 us (46%)
  starting transfers between devices  59.6 us (27%)
  waiting for transfers between devices  33.4 us (15%)
  other arithmetic  9.98 us (5%)
  local copies, waits for them, and re-layouts  9.68 us (4%)
  matrix products  4.63 us (2%)
    psum x1, blocking collectives, local(): gram_matrix, rayleigh = lax.psum((gram_part, rayleigh_part), 'rows')  62.2 us
    ppermute x15, starting transfers between devices, rotated_exchange(): lax.ppermute(sent, axis, [(d, (d + far) % ways) for d in range(ways)])  40.8 us
    psum x1, blocking collectives, local(): squares = lax.psum(jnp.sum(smooth * smooth, axis=1), 'rows')  32.1 us
    ppermute x15, waiting for transfers between devices, rotated_exchange(): lax.ppermute(sent, axis, [(d, (d + far) % ways) for d in range(ways)])  17.3 us
    all_to_all x1, waiting for transfers between devices, local(): lax.all_to_all(to_slots(remain, owner_dev, row_devices), 'rows', split_ax...  7.32 us
    ppermute x4, waiting for transfers between devices, extended(): after = lax.ppermute(initial, axis, down)  6.72 us
    ppermute x4, starting transfers between devices, extended(): before = lax.ppermute(last, axis, up)  6.26 us
    all_gather x1, blocking collectives, local(): all_states = lax.all_gather(states, 'cols', axis=0, tiled=True)  5.51 us
  transfers between devices with their start and end apart: 25, of which 14 were waited for; matrix products, arithmetic and copies ran while one was open for 4% of the time, Pallas kernels for 0%

profile of v1, /device:TPU:0, one launch (start us, length us, event | category | flops | bytes accessed | tf_op | source)
XLA Modules:
  0.0 217.7 jit_solution(16097915560305221612)
XLA Ops:
  0.8 2.4 %collective-permute-start = (f32[16,512]{1,0:T(8,128)S(1)}, f32[16,512]{1,0:T(8,128)S(1)}, u32[]{:S(2)}, u32[]{:S(2)}) collective-permute-start(f32[16,512]{1,0:T(8,128)S(1)} %get-tuple-element.31), channel_id=1, source_target_pairs={{0,2},{2,4},{4,6},{6,8},{8,10},{10,12},{12,14},{14,16},{16,18},{18... | collective-permute-start | bytes 98312 | tf_op jit(solution)/shard_map/ppermute | solution.py:30
  4.5 5.5 %all_gather.3 = f32[32,1024]{1,0:T(8,128)S(1)} all-gather(f32[16,1024]{1,0:T(8,128)} %param.6), channel_id=1, replica_groups=mesh['rows'=16,'cols'=2] {'cols'}, dimensions={0}, use_global_device_ids=true | all-gather | bytes 196608 | tf_op jit(solution)/shard_map/all_gather | solution.py:75
  10.9 1.4 convert_reduce_fusion
  14.4 62.2 %all-reduce = (f32[32,16]{0,1:T(8,128)S(1)}, f32[32,32]{0,1:T(8,128)S(1)}) all-reduce(f32[32,16]{0,1:T(8,128)S(1)} %convolution_bitcast_fusion.4, f32[32,32]{0,1:T(8,128)S(1)} %fusion.1), channel_id=1, replica_groups=mesh['rows'=16,'cols'=2] {'rows'}, use_global_device_ids=true, to_apply=%region_4.5 | all-reduce | flops 1536 | bytes 12288 | tf_op jit(solution)/shard_map/psum | solution.py:78
  76.7 2.9 %cholesky.16 = f32[32,32]{1,0:T(8,128)S(1)} custom-call(f32[32,32]{1,0:T(8,128)S(1)} %fusion.22), custom_call_target="Cholesky" | custom-call | tf_op jit(solution)/shard_map/jit(cholesky)/cholesky | solution.py:46
  81.0 2.4 %custom-call.10 = f32[1,32,32]{1,2,0:T(8,128)S(1)} custom-call(f32[1,32,32]{2,1,0:T(8,128)S(1)} %fusion.17), custom_call_target="InvertDiagBlocksLowerTriangular" | custom-call | tf_op jit(solution)/shard_map/jit(_cho_solve)/triangular_solve | solution.py:47
  87.7 3.5 %all-to-all-start.1 = ((f32[1,16,128]{2,0,1:T(1,128)}), f32[1,16,128]{2,0,1:T(1,128)S(1)}, u32[]{:S(2)}, u32[]{:S(2)}) async-start(f32[1,16,128]{2,0,1:T(1,128)} %bitcast.17), calls=%async_computation.1 | async-start | bytes 16384 | tf_op jit(solution)/shard_map/all_to_all | solution.py:91
  93.5 2.0 scatter_fusion
  95.4 2.1 all-to-all-done.1
  97.5 3.9 %all-to-all-start = ((f32[16,16,128]{2,0,1:T(8,128)}), f32[16,16,128]{2,0,1:T(8,128)S(1)}, u32[]{:S(2)}, u32[]{:S(2)}) async-start(f32[16,16,128]{2,0,1:T(8,128)} %scatter_fusion), calls=%async_computation | async-start | bytes 262144 | tf_op jit(solution)/shard_map/all_to_all | solution.py:84
  102.0 7.3 %all-to-all-done = f32[16,16,128]{2,0,1:T(8,128)S(1)} async-done(((f32[16,16,128]{2,0,1:T(8,128)}), f32[16,16,128]{2,0,1:T(8,128)S(1)}, u32[]{:S(2)}, u32[]{:S(2)}) %all-to-all-start) | async-done | bytes 131104 | tf_op jit(solution)/shard_map/all_to_all | solution.py:84
  112.6 1.8 collective-permute-done.5
  116.7 1.6 collective-permute-start.6
  119.1 2.4 %collective-permute-start.19 = (f32[16,1,128]{2,0,1:T(8,128)S(1)}, f32[16,1,128]{2,0,1:T(8,128)S(1)}, u32[]{:S(2)}, u32[]{:S(2)}) collective-permute-start(f32[16,1,128]{2,0,1:T(8,128)S(1)} %get-tuple-element.11), channel_id=1, source_target_pairs={{0,4},{2,6},{4,8},{6,10},{8,12},{10,14},{12,16},{14,18},{16,20},{1... | collective-permute-start | bytes 24584 | tf_op jit(solution)/shard_map/ppermute | solution.py:18
  121.5 2.2 collective-permute-start.18
  123.6 1.6 collective-permute-start.17
  125.2 4.4 %collective-permute-start.7 = (f32[16,1,128]{2,0,1:T(8,128)S(1)}, f32[16,1,128]{2,0,1:T(8,128)S(1)}, u32[]{:S(2)}, u32[]{:S(2)}) collective-permute-start(f32[16,1,128]{2,0,1:T(8,128)S(1)} %get-tuple-element.23), channel_id=1, source_target_pairs={{0,28},{2,30},{4,0},{6,2},{8,4},{10,6},{12,8},{14,10},{16,12},{18,... | collective-permute-start | bytes 24584 | tf_op jit(solution)/shard_map/ppermute | solution.py:18
  129.7 1.4 collective-permute-done.7
  131.1 3.1 %collective-permute-done.8 = f32[16,1,128]{2,0,1:T(8,128)S(1)} collective-permute-done((f32[16,1,128]{2,0,1:T(8,128)S(1)}, f32[16,1,128]{2,0,1:T(8,128)S(1)}, u32[]{:S(2)}, u32[]{:S(2)}) %collective-permute-start.8) | collective-permute-done | bytes 8224 | tf_op jit(solution)/shard_map/ppermute | solution.py:18
  135.3 2.5 %collective-permute-done.9 = f32[16,1,128]{2,0,1:T(8,128)S(1)} collective-permute-done((f32[16,1,128]{2,0,1:T(8,128)S(1)}, f32[16,1,128]{2,0,1:T(8,128)S(1)}, u32[]{:S(2)}, u32[]{:S(2)}) %collective-permute-start.9) | collective-permute-done | bytes 8224 | tf_op jit(solution)/shard_map/ppermute | solution.py:18
  137.8 2.4 %collective-permute-start.10 = (f32[16,1,128]{2,0,1:T(8,128)S(1)}, f32[16,1,128]{2,0,1:T(8,128)S(1)}, u32[]{:S(2)}, u32[]{:S(2)}) collective-permute-start(f32[16,1,128]{2,0,1:T(8,128)S(1)} %get-tuple-element.20), channel_id=1, source_target_pairs={{0,22},{2,24},{4,26},{6,28},{8,30},{10,0},{12,2},{14,4},{16,6},{18... | collective-permute-start | bytes 24584 | tf_op jit(solution)/shard_map/ppermute | solution.py:18
  140.2 1.4 collective-permute-done.10
  141.5 5.6 %collective-permute-start.11 = (f32[16,1,128]{2,0,1:T(8,128)S(1)}, f32[16,1,128]{2,0,1:T(8,128)S(1)}, u32[]{:S(2)}, u32[]{:S(2)}) collective-permute-start(f32[16,1,128]{2,0,1:T(8,128)S(1)} %get-tuple-element.19), channel_id=1, source_target_pairs={{0,20},{2,22},{4,24},{6,26},{8,28},{10,30},{12,0},{14,2},{16,4},{1... | collective-permute-start | bytes 24584 | tf_op jit(solution)/shard_map/ppermute | solution.py:18
  148.4 3.8 %collective-permute-start.12 = (f32[16,1,128]{2,0,1:T(8,128)S(1)}, f32[16,1,128]{2,0,1:T(8,128)S(1)}, u32[]{:S(2)}, u32[]{:S(2)}) collective-permute-start(f32[16,1,128]{2,0,1:T(8,128)S(1)} %get-tuple-element.18), channel_id=1, source_target_pairs={{0,18},{2,20},{4,22},{6,24},{8,26},{10,28},{12,30},{14,0},{16,2},{... | collective-permute-start | bytes 24584 | tf_op jit(solution)/shard_map/ppermute | solution.py:18
  153.6 4.7 %collective-permute-start.13 = (f32[16,1,128]{2,0,1:T(8,128)S(1)}, f32[16,1,128]{2,0,1:T(8,128)S(1)}, u32[]{:S(2)}, u32[]{:S(2)}) collective-permute-start(f32[16,1,128]{2,0,1:T(8,128)S(1)} %get-tuple-element.17), channel_id=1, source_target_pairs={{0,16},{2,18},{4,20},{6,22},{8,24},{10,26},{12,28},{14,30},{16,0},... | collective-permute-start | bytes 24584 | tf_op jit(solution)/shard_map/ppermute | solution.py:18
  158.3 1.6 collective-permute-done.13
  159.9 2.7 %collective-permute-start.14 = (f32[16,1,128]{2,0,1:T(8,128)S(1)}, f32[16,1,128]{2,0,1:T(8,128)S(1)}, u32[]{:S(2)}, u32[]{:S(2)}) collective-permute-start(f32[16,1,128]{2,0,1:T(8,128)S(1)} %get-tuple-element.16), channel_id=1, source_target_pairs={{0,14},{2,16},{4,18},{6,20},{8,22},{10,24},{12,26},{14,28},{16,30}... | collective-permute-start | bytes 24584 | tf_op jit(solution)/shard_map/ppermute | solution.py:18
  164.0 4.7 %collective-permute-start.15 = (f32[16,1,128]{2,0,1:T(8,128)S(1)}, f32[16,1,128]{2,0,1:T(8,128)S(1)}, u32[]{:S(2)}, u32[]{:S(2)}) collective-permute-start(f32[16,1,128]{2,0,1:T(8,128)S(1)} %get-tuple-element.15), channel_id=1, source_target_pairs={{0,12},{2,14},{4,16},{6,18},{8,20},{10,22},{12,24},{14,26},{16,28}... | collective-permute-start | bytes 24584 | tf_op jit(solution)/shard_map/ppermute | solution.py:18
  170.0 2.9 %collective-permute-start.16 = (f32[16,1,128]{2,0,1:T(8,128)S(1)}, f32[16,1,128]{2,0,1:T(8,128)S(1)}, u32[]{:S(2)}, u32[]{:S(2)}) collective-permute-start(f32[16,1,128]{2,0,1:T(8,128)S(1)} %get-tuple-element.14), channel_id=1, source_target_pairs={{0,10},{2,12},{4,14},{6,16},{8,18},{10,20},{12,22},{14,24},{16,26}... | collective-permute-start | bytes 24584 | tf_op jit(solution)/shard_map/ppermute | solution.py:18
  172.9 1.9 collective-permute-done.16
  178.2 4.9 %collective-permute-done.22 = f32[16,512]{1,0:T(8,128)S(1)} collective-permute-done((f32[16,512]{1,0:T(8,128)S(1)}, f32[16,512]{1,0:T(8,128)S(1)}, u32[]{:S(2)}, u32[]{:S(2)}) %collective-permute-start.22) | collective-permute-done | bytes 32800 | tf_op jit(solution)/shard_map/ppermute | solution.py:31
  184.9 32.1 %psum.23 = f32[16]{0:T(128)S(1)} all-reduce(f32[16]{0:T(128)S(1)} %get-tuple-element.8), channel_id=1, replica_groups=mesh['rows'=16,'cols'=2] {'rows'}, use_global_device_ids=true, to_apply=%region_9.11 | all-reduce | flops 16 | bytes 128 | tf_op jit(solution)/shard_map/psum | solution.py:108
  (97 shorter events, 32.0 us)
Async XLA Ops:
  0.0 12.6 %copy-start.1 = (f32[16,1024]{1,0:T(8,128)S(1)}, f32[16,1024]{1,0:T(8,128)}, u32[]{:S(2)}) copy-start(f32[16,1024]{1,0:T(8,128)} %param.6) | copy-start | bytes 196612
  0.8 11.8 %collective-permute-start = (f32[16,512]{1,0:T(8,128)S(1)}, f32[16,512]{1,0:T(8,128)S(1)}, u32[]{:S(2)}, u32[]{:S(2)}) collective-permute-start(f32[16,512]{1,0:T(8,128)S(1)} %get-tuple-element.31), channel_id=1, source_target_pairs={{0,2},{2,4},{4,6},{6,8},{8,10},{10,12},{12,14},{14,16},{16,18},{18... | collective-permute-start | bytes 98312 | tf_op jit(solution)/shard_map/ppermute | solution.py:30
  3.2 9.4 %collective-permute-start.1 = (f32[16,512]{1,0:T(8,128)S(1)}, f32[16,512]{1,0:T(8,128)S(1)}, u32[]{:S(2)}, u32[]{:S(2)}) collective-permute-start(f32[16,512]{1,0:T(8,128)S(1)} %get-tuple-element.32), channel_id=1, source_target_pairs={{2,0},{4,2},{6,4},{8,6},{10,8},{12,10},{14,12},{16,14},{18,16},{20... | collective-permute-start | bytes 98312 | tf_op jit(solution)/shard_map/ppermute | solution.py:31
  10.9 2.3 %copy-start = (bf16[8,3,128,128]{3,2,1,0:T(8,128)(2,1)S(1)}, bf16[8,3,128,128]{3,2,1,0:T(8,128)(2,1)}, u32[]{:S(2)}) copy-start(bf16[8,3,128,128]{3,2,1,0:T(8,128)(2,1)} %param.7) | copy-start | bytes 2359300
  14.2 72.4 %copy-start.2 = (s32[8]{0:T(128)S(1)}, s32[8]{0:T(128)}, u32[]{:S(2)}) copy-start(s32[8]{0:T(128)} %param.9) | copy-start | bytes 100
  83.9 7.3 %collective-permute-start.2 = (f32[16,512]{1,0:T(8,128)S(1)}, f32[16,512]{1,0:T(8,128)S(1)}, u32[]{:S(2)}, u32[]{:S(2)}) collective-permute-start(f32[16,512]{1,0:T(8,128)S(1)} %get-tuple-element.29), channel_id=1, source_target_pairs={{0,2},{2,4},{4,6},{6,8},{8,10},{10,12},{12,14},{14,16},{16,18},{18... | collective-permute-start | bytes 98312 | tf_op jit(solution)/shard_map/ppermute | solution.py:30
  85.2 6.0 %collective-permute-start.3 = (f32[16,512]{1,0:T(8,128)S(1)}, f32[16,512]{1,0:T(8,128)S(1)}, u32[]{:S(2)}, u32[]{:S(2)}) collective-permute-start(f32[16,512]{1,0:T(8,128)S(1)} %get-tuple-element.30), channel_id=1, source_target_pairs={{2,0},{4,2},{6,4},{8,6},{10,8},{12,10},{14,12},{16,14},{18,16},{20... | collective-permute-start | bytes 98312 | tf_op jit(solution)/shard_map/ppermute | solution.py:31
  87.7 9.8 %all-to-all-start.1 = ((f32[1,16,128]{2,0,1:T(1,128)}), f32[1,16,128]{2,0,1:T(1,128)S(1)}, u32[]{:S(2)}, u32[]{:S(2)}) async-start(f32[1,16,128]{2,0,1:T(1,128)} %bitcast.17), calls=%async_computation.1 | async-start | bytes 16384 | tf_op jit(solution)/shard_map/all_to_all | solution.py:91
  97.5 11.8 %all-to-all-start = ((f32[16,16,128]{2,0,1:T(8,128)}), f32[16,16,128]{2,0,1:T(8,128)S(1)}, u32[]{:S(2)}, u32[]{:S(2)}) async-start(f32[16,16,128]{2,0,1:T(8,128)} %scatter_fusion), calls=%async_computation | async-start | bytes 262144 | tf_op jit(solution)/shard_map/all_to_all | solution.py:84
  109.9 2.6 %collective-permute-start.4 = (f32[16,512]{1,0:T(8,128)S(1)}, f32[16,512]{1,0:T(8,128)S(1)}, u32[]{:S(2)}, u32[]{:S(2)}) collective-permute-start(f32[16,512]{1,0:T(8,128)S(1)} %get-tuple-element.27), channel_id=1, source_target_pairs={{0,2},{2,4},{4,6},{6,8},{8,10},{10,12},{12,14},{14,16},{16,18},{18... | collective-permute-start | bytes 98312 | tf_op jit(solution)/shard_map/ppermute | solution.py:30
  111.2 3.1 %collective-permute-start.5 = (f32[16,512]{1,0:T(8,128)S(1)}, f32[16,512]{1,0:T(8,128)S(1)}, u32[]{:S(2)}, u32[]{:S(2)}) collective-permute-start(f32[16,512]{1,0:T(8,128)S(1)} %get-tuple-element.28), channel_id=1, source_target_pairs={{2,0},{4,2},{6,4},{8,6},{10,8},{12,10},{14,12},{16,14},{18,16},{20... | collective-permute-start | bytes 98312 | tf_op jit(solution)/shard_map/ppermute | solution.py:31
  116.7 8.5 %collective-permute-start.6 = (f32[16,1,128]{2,0,1:T(8,128)S(1)}, f32[16,1,128]{2,0,1:T(8,128)S(1)}, u32[]{:S(2)}, u32[]{:S(2)}) collective-permute-start(f32[16,1,128]{2,0,1:T(8,128)S(1)} %get-tuple-element.24), channel_id=1, source_target_pairs={{0,30},{2,0},{4,2},{6,4},{8,6},{10,8},{12,10},{14,12},{16,14},{18,... | collective-permute-start | bytes 24584 | tf_op jit(solution)/shard_map/ppermute | solution.py:18
  118.4 56.6 %collective-permute-start.20 = (f32[16,1,128]{2,0,1:T(8,128)S(1)}, f32[16,1,128]{2,0,1:T(8,128)S(1)}, u32[]{:S(2)}, u32[]{:S(2)}) collective-permute-start(f32[16,1,128]{2,0,1:T(8,128)S(1)} %get-tuple-element.10), channel_id=1, source_target_pairs={{0,2},{2,4},{4,6},{6,8},{8,10},{10,12},{12,14},{14,16},{16,18},{18... | collective-permute-start | bytes 24584 | tf_op jit(solution)/shard_map/ppermute | solution.py:18
  119.1 55.8 %collective-permute-start.19 = (f32[16,1,128]{2,0,1:T(8,128)S(1)}, f32[16,1,128]{2,0,1:T(8,128)S(1)}, u32[]{:S(2)}, u32[]{:S(2)}) collective-permute-start(f32[16,1,128]{2,0,1:T(8,128)S(1)} %get-tuple-element.11), channel_id=1, source_target_pairs={{0,4},{2,6},{4,8},{6,10},{8,12},{10,14},{12,16},{14,18},{16,20},{1... | collective-permute-start | bytes 24584 | tf_op jit(solution)/shard_map/ppermute | solution.py:18
  121.5 53.4 %collective-permute-start.18 = (f32[16,1,128]{2,0,1:T(8,128)S(1)}, f32[16,1,128]{2,0,1:T(8,128)S(1)}, u32[]{:S(2)}, u32[]{:S(2)}) collective-permute-start(f32[16,1,128]{2,0,1:T(8,128)S(1)} %get-tuple-element.12), channel_id=1, source_target_pairs={{0,6},{2,8},{4,10},{6,12},{8,14},{10,16},{12,18},{14,20},{16,22},{... | collective-permute-start | bytes 24584 | tf_op jit(solution)/shard_map/ppermute | solution.py:18
  123.6 51.2 %collective-permute-start.17 = (f32[16,1,128]{2,0,1:T(8,128)S(1)}, f32[16,1,128]{2,0,1:T(8,128)S(1)}, u32[]{:S(2)}, u32[]{:S(2)}) collective-permute-start(f32[16,1,128]{2,0,1:T(8,128)S(1)} %get-tuple-element.13), channel_id=1, source_target_pairs={{0,8},{2,10},{4,12},{6,14},{8,16},{10,18},{12,20},{14,22},{16,24},... | collective-permute-start | bytes 24584 | tf_op jit(solution)/shard_map/ppermute | solution.py:18
  125.2 5.8 %collective-permute-start.7 = (f32[16,1,128]{2,0,1:T(8,128)S(1)}, f32[16,1,128]{2,0,1:T(8,128)S(1)}, u32[]{:S(2)}, u32[]{:S(2)}) collective-permute-start(f32[16,1,128]{2,0,1:T(8,128)S(1)} %get-tuple-element.23), channel_id=1, source_target_pairs={{0,28},{2,30},{4,0},{6,2},{8,4},{10,6},{12,8},{14,10},{16,12},{18,... | collective-permute-start | bytes 24584 | tf_op jit(solution)/shard_map/ppermute | solution.py:18
  131.1 3.1 %collective-permute-start.8 = (f32[16,1,128]{2,0,1:T(8,128)S(1)}, f32[16,1,128]{2,0,1:T(8,128)S(1)}, u32[]{:S(2)}, u32[]{:S(2)}) collective-permute-start(f32[16,1,128]{2,0,1:T(8,128)S(1)} %get-tuple-element.22), channel_id=1, source_target_pairs={{0,26},{2,28},{4,30},{6,0},{8,2},{10,4},{12,6},{14,8},{16,10},{18,... | collective-permute-start | bytes 24584 | tf_op jit(solution)/shard_map/ppermute | solution.py:18
  134.1 3.7 %collective-permute-start.9 = (f32[16,1,128]{2,0,1:T(8,128)S(1)}, f32[16,1,128]{2,0,1:T(8,128)S(1)}, u32[]{:S(2)}, u32[]{:S(2)}) collective-permute-start(f32[16,1,128]{2,0,1:T(8,128)S(1)} %get-tuple-element.21), channel_id=1, source_target_pairs={{0,24},{2,26},{4,28},{6,30},{8,0},{10,2},{12,4},{14,6},{16,8},{18,... | collective-permute-start | bytes 24584 | tf_op jit(solution)/shard_map/ppermute | solution.py:18
  137.8 3.7 %collective-permute-start.10 = (f32[16,1,128]{2,0,1:T(8,128)S(1)}, f32[16,1,128]{2,0,1:T(8,128)S(1)}, u32[]{:S(2)}, u32[]{:S(2)}) collective-permute-start(f32[16,1,128]{2,0,1:T(8,128)S(1)} %get-tuple-element.20), channel_id=1, source_target_pairs={{0,22},{2,24},{4,26},{6,28},{8,30},{10,0},{12,2},{14,4},{16,6},{18... | collective-permute-start | bytes 24584 | tf_op jit(solution)/shard_map/ppermute | solution.py:18
  141.5 6.9 %collective-permute-start.11 = (f32[16,1,128]{2,0,1:T(8,128)S(1)}, f32[16,1,128]{2,0,1:T(8,128)S(1)}, u32[]{:S(2)}, u32[]{:S(2)}) collective-permute-start(f32[16,1,128]{2,0,1:T(8,128)S(1)} %get-tuple-element.19), channel_id=1, source_target_pairs={{0,20},{2,22},{4,24},{6,26},{8,28},{10,30},{12,0},{14,2},{16,4},{1... | collective-permute-start | bytes 24584 | tf_op jit(solution)/shard_map/ppermute | solution.py:18
  148.4 5.2 %collective-permute-start.12 = (f32[16,1,128]{2,0,1:T(8,128)S(1)}, f32[16,1,128]{2,0,1:T(8,128)S(1)}, u32[]{:S(2)}, u32[]{:S(2)}) collective-permute-start(f32[16,1,128]{2,0,1:T(8,128)S(1)} %get-tuple-element.18), channel_id=1, source_target_pairs={{0,18},{2,20},{4,22},{6,24},{8,26},{10,28},{12,30},{14,0},{16,2},{... | collective-permute-start | bytes 24584 | tf_op jit(solution)/shard_map/ppermute | solution.py:18
  153.6 6.3 %collective-permute-start.13 = (f32[16,1,128]{2,0,1:T(8,128)S(1)}, f32[16,1,128]{2,0,1:T(8,128)S(1)}, u32[]{:S(2)}, u32[]{:S(2)}) collective-permute-start(f32[16,1,128]{2,0,1:T(8,128)S(1)} %get-tuple-element.17), channel_id=1, source_target_pairs={{0,16},{2,18},{4,20},{6,22},{8,24},{10,26},{12,28},{14,30},{16,0},... | collective-permute-start | bytes 24584 | tf_op jit(solution)/shard_map/ppermute | solution.py:18
  159.9 4.0 %collective-permute-start.14 = (f32[16,1,128]{2,0,1:T(8,128)S(1)}, f32[16,1,128]{2,0,1:T(8,128)S(1)}, u32[]{:S(2)}, u32[]{:S(2)}) collective-permute-start(f32[16,1,128]{2,0,1:T(8,128)S(1)} %get-tuple-element.16), channel_id=1, source_target_pairs={{0,14},{2,16},{4,18},{6,20},{8,22},{10,24},{12,26},{14,28},{16,30}... | collective-permute-start | bytes 24584 | tf_op jit(solution)/shard_map/ppermute | solution.py:18
  164.0 6.0 %collective-permute-start.15 = (f32[16,1,128]{2,0,1:T(8,128)S(1)}, f32[16,1,128]{2,0,1:T(8,128)S(1)}, u32[]{:S(2)}, u32[]{:S(2)}) collective-permute-start(f32[16,1,128]{2,0,1:T(8,128)S(1)} %get-tuple-element.15), channel_id=1, source_target_pairs={{0,12},{2,14},{4,16},{6,18},{8,20},{10,22},{12,24},{14,26},{16,28}... | collective-permute-start | bytes 24584 | tf_op jit(solution)/shard_map/ppermute | solution.py:18
  170.0 4.9 %collective-permute-start.16 = (f32[16,1,128]{2,0,1:T(8,128)S(1)}, f32[16,1,128]{2,0,1:T(8,128)S(1)}, u32[]{:S(2)}, u32[]{:S(2)}) collective-permute-start(f32[16,1,128]{2,0,1:T(8,128)S(1)} %get-tuple-element.14), channel_id=1, source_target_pairs={{0,10},{2,12},{4,14},{6,16},{8,18},{10,20},{12,22},{14,24},{16,26}... | collective-permute-start | bytes 24584 | tf_op jit(solution)/shard_map/ppermute | solution.py:18
  175.6 2.6 %collective-permute-start.21 = (f32[16,512]{1,0:T(8,128)S(1)}, f32[16,512]{1,0:T(8,128)S(1)}, u32[]{:S(2)}, u32[]{:S(2)}) collective-permute-start(f32[16,512]{1,0:T(8,128)S(1)} %get-tuple-element.25), channel_id=1, source_target_pairs={{0,2},{2,4},{4,6},{6,8},{8,10},{10,12},{12,14},{14,16},{16,18},{18... | collective-permute-start | bytes 98312 | tf_op jit(solution)/shard_map/ppermute | solution.py:30
  176.9 6.3 %collective-permute-start.22 = (f32[16,512]{1,0:T(8,128)S(1)}, f32[16,512]{1,0:T(8,128)S(1)}, u32[]{:S(2)}, u32[]{:S(2)}) collective-permute-start(f32[16,512]{1,0:T(8,128)S(1)} %get-tuple-element.26), channel_id=1, source_target_pairs={{2,0},{4,2},{6,4},{8,6},{10,8},{12,10},{14,12},{16,14},{18,16},{20... | collective-permute-start | bytes 98312 | tf_op jit(solution)/shard_map/ppermute | solution.py:31
